TPU v7x, 32 devices: a whole 2x2x4 slice. The times are simulated.
32 devices in a mesh: row: 2 (over y), col: 8 (over z, core), orient: 2 (over x).
Axes of the slice: x: 2, y: 2, z: 4, core: 2. Of those that a mesh axis runs over, the one named last changes fastest.
Arguments:
- noise: float32 [2, 4096, 4096], P(None, ('row', 'col')), may hold values from -6 to 6
- elevation_library: float32 [16, 128, 128], replicated, may hold values from 0.25 to 1
- tile_choice_index: int32 [32, 32], P('row', 'col'), may hold values from 0 to 15
- family_heading_index: int32 [8], P('orient'), may hold values from 0 to 35
- family_extent_index: int32 [8], P('orient'), may hold values from 0 to 3
Outputs:
- safety_min: float32 [4096, 4096], P('row', ('col', 'orient'))
All inputs are finite; a program needn't handle non-finite values.
Results may differ from a plain program's by a relative error of at most 0.0005.
Values may be sent and summed in bfloat16 or wider, within the bound.
A program may use at most 256 MiB of HBM per device.

v0:
```python
import math
import jax
import jax.numpy as jnp
from jax import lax
from jax.sharding import PartitionSpec as P

R = 8
N_AZ = 36
NSIZE = 4
nugget_share = 0.3
peak_share = 1024.0 / (2.0 * math.pi)
cutoff_ratio = 32.0


def extended(cells, sides, width):
    for axis, dim in sides:
        count = lax.axis_size(axis)
        ends = count - 1
        head = lax.slice_in_dim(cells, 0, width, axis=dim)
        tail = lax.slice_in_dim(cells, cells.shape[dim] - width, cells.shape[dim], axis=dim)
        cells = jnp.concatenate(
            [
                lax.ppermute(tail, axis, [(i, (i + 1) % count) for i in range(ends)]),
                cells,
                lax.ppermute(head, axis, [((i + 1) % count, i) for i in range(ends)]),
            ],
            axis=dim,
        )
    return cells


def partner(x, axis, bit):
    return lax.ppermute(x, axis, [(i, i ^ 1 << bit) for i in range(lax.axis_size(axis))])


def amplitude(u_index, v_index, side_cells):
    wrap_u = jnp.minimum(u_index, side_cells - u_index).astype(jnp.float32)
    wrap_v = jnp.minimum(v_index, side_cells - v_index).astype(jnp.float32)
    cutoff = side_cells / cutoff_ratio
    scaled_u = wrap_u / cutoff
    scaled_v = wrap_v / cutoff
    grown = 1.0 + scaled_u * scaled_u + scaled_v * scaled_v
    spectrum = nugget_share + peak_share / (grown * jnp.sqrt(grown))
    return jnp.sqrt(spectrum) / side_cells


def ellipsoid(offset_u, offset_v, azimuth, size_index):
    heading = azimuth.astype(jnp.float32) * (math.pi / N_AZ)
    semi_axis = R * (size_index.astype(jnp.float32) + (1 + NSIZE)) / (2 * NSIZE)
    across = 0.6 * semi_axis
    slip_depth = 0.3 * semi_axis
    along = offset_u * jnp.cos(heading) + offset_v * jnp.sin(heading)
    lateral = offset_v * jnp.cos(heading) - offset_u * jnp.sin(heading)
    along_part = along / semi_axis
    lateral_part = lateral / across
    inside = 1.0 - along_part * along_part - lateral_part * lateral_part
    height = slip_depth * jnp.sqrt(jnp.maximum(inside, 0.0))
    base_share = jnp.clip(4.0 * inside, 0.0, 1.0)
    return (height, base_share)


def angle_table(row_count, col_count, period):
    left_index = lax.broadcasted_iota(jnp.int32, (row_count, col_count), 0)
    right_index = lax.broadcasted_iota(jnp.int32, (row_count, col_count), 1)
    phase_step = left_index * right_index % period
    angles = phase_step.astype(jnp.float32) * (2.0 * math.pi / period)
    return (jnp.cos(angles), jnp.sin(angles))


def transform_last(real_part, imag_part):
    length = real_part.shape[-1]
    inner_size = 128
    outer_size = length // inner_size
    leading = real_part.shape[:-1]
    real_in = real_part.reshape(leading + (outer_size, inner_size))
    imag_in = imag_part.reshape(leading + (outer_size, inner_size))
    highest = lax.Precision.HIGHEST
    outer_cos, outer_sin = angle_table(outer_size, outer_size, outer_size)
    real_mid = jnp.einsum("...pq,pk->...kq", real_in, outer_cos, precision=highest) + jnp.einsum(
        "...pq,pk->...kq", imag_in, outer_sin, precision=highest
    )
    imag_mid = jnp.einsum("...pq,pk->...kq", imag_in, outer_cos, precision=highest) - jnp.einsum(
        "...pq,pk->...kq", real_in, outer_sin, precision=highest
    )
    twist_cos, twist_sin = angle_table(outer_size, inner_size, length)
    real_twist = real_mid * twist_cos + imag_mid * twist_sin
    imag_twist = imag_mid * twist_cos - real_mid * twist_sin
    inner_cos, inner_sin = angle_table(inner_size, inner_size, inner_size)
    real_out = jnp.einsum("...kq,ql->...kl", real_twist, inner_cos, precision=highest) + jnp.einsum(
        "...kq,ql->...kl", imag_twist, inner_sin, precision=highest
    )
    imag_out = jnp.einsum("...kq,ql->...kl", imag_twist, inner_cos, precision=highest) - jnp.einsum(
        "...kq,ql->...kl", real_twist, inner_sin, precision=highest
    )
    real_out = jnp.swapaxes(real_out, -1, -2).reshape(leading + (length,))
    imag_out = jnp.swapaxes(imag_out, -1, -2).reshape(leading + (length,))
    return (real_out, imag_out)


def body(noise, elevation_library, tile_choice_index, family_heading_index, family_extent_index):
    line_count = noise.shape[1]
    side_cells = noise.shape[2]
    first_line = lax.axis_index(("row", "col")) * line_count
    v_index = first_line + lax.broadcasted_iota(jnp.int32, (line_count, side_cells), 0)
    u_index = lax.broadcasted_iota(jnp.int32, (line_count, side_cells), 1)
    amplitudes = amplitude(u_index, v_index, side_cells)
    real_part, imag_part = transform_last(noise[0] * amplitudes, noise[1] * amplitudes)
    spectrum = jnp.stack([real_part, imag_part])
    transposed = lax.all_to_all(
        spectrum.astype(jnp.bfloat16), ("row", "col"), split_axis=2, concat_axis=1, tiled=True
    ).astype(spectrum.dtype)
    turned = jnp.swapaxes(transposed, 1, 2)
    field_re, field_im = transform_last(turned[0], turned[1])
    fields = lax.all_to_all(
        jnp.stack([field_re, field_im]).astype(jnp.bfloat16),
        "col",
        split_axis=2,
        concat_axis=1,
        tiled=True,
    ).astype(jnp.float32)
    window_rows = fields.shape[1]
    window_columns = fields.shape[2]
    elevation_tiles = jnp.take(elevation_library, tile_choice_index, axis=0)
    slope_tangents = elevation_tiles.transpose(0, 2, 1, 3).reshape(window_rows, window_columns)
    secant = jnp.sqrt(1.0 + slope_tangents * slope_tangents)
    cohesion = 0.5 * jnp.exp(0.4 * fields[0])
    friction = 0.6 * jnp.exp(0.25 * fields[1])
    column_terms = jnp.stack(
        [cohesion * secant, friction / secant, slope_tangents / secant]
    ).astype(jnp.bfloat16)
    padded = extended(column_terms, (("row", 1), ("col", 2)), R)
    tile_width = min(128, window_columns)
    tile_count = window_columns // tile_width
    strip_span = tile_width + 2 * R
    strips = jnp.stack(
        [
            padded[:, :, tile_index * tile_width : tile_index * tile_width + strip_span]
            for tile_index in range(tile_count)
        ],
        axis=2,
    )
    kernel_width = 2 * R + 1
    shift_index = lax.broadcasted_iota(jnp.int32, (kernel_width, strip_span, tile_width), 0)
    strip_index = lax.broadcasted_iota(jnp.int32, (kernel_width, strip_span, tile_width), 1)
    out_index = lax.broadcasted_iota(jnp.int32, (kernel_width, strip_span, tile_width), 2)
    column_gap = strip_index - out_index
    offset_u = (shift_index - R).astype(jnp.float32)
    offset_v = (column_gap - R).astype(jnp.float32)
    inside_band = (column_gap >= 0) & (column_gap <= 2 * R)
    height, base_share = ellipsoid(
        offset_u[None],
        offset_v[None],
        family_heading_index[:, None, None, None],
        family_extent_index[:, None, None, None],
    )
    band_height = jnp.where(inside_band[None], height, 0.0).astype(jnp.bfloat16)
    band_share = jnp.where(inside_band[None], base_share, 0.0).astype(jnp.bfloat16)
    shifted = jnp.stack(
        [strips[:, row_shift : row_shift + window_rows] for row_shift in range(kernel_width)],
        axis=1,
    )
    resist_kernel = jnp.stack([band_share, band_height])
    resisting = jnp.einsum(
        "csxti,cfsio->fxto", shifted[0:2], resist_kernel, preferred_element_type=jnp.float32
    )
    driving = jnp.einsum(
        "sxti,fsio->fxto", shifted[2], band_height, preferred_element_type=jnp.float32
    )
    safety = resisting / driving
    family_low = jnp.min(safety, axis=0).reshape(window_rows, window_columns)
    half_width = window_columns // 2
    side_index = lax.axis_index("orient")
    own_half = lax.dynamic_slice_in_dim(family_low, side_index * half_width, half_width, 1)
    other_half = lax.dynamic_slice_in_dim(family_low, (1 - side_index) * half_width, half_width, 1)
    partner_half = partner(other_half, "orient", 0)
    return jnp.minimum(own_half, partner_half)


def solution(mesh):
    placed = (P(None, ("row", "col"), None), P(), P("row", "col"), P("orient"), P("orient"))
    return jax.shard_map(
        body, mesh=mesh, in_specs=placed, out_specs=P("row", ("col", "orient")), check_vma=False
    )
```

profile of v0, /device:TPU:0, one launch (start us, length us, event | category | flops | bytes accessed | tf_op | source)
XLA Modules:
  0.0 706.0 jit_solution(4212948183642729390)
XLA Ops:
  33.8 7.0 fusion.40
  48.7 6.8 fusion.61
  57.0 25.5 %copy.105 = bf16[2,256,4096]{1,0,2:T(2,128)(2,1)S(1)} copy(bf16[2,256,4096]{1,2,0:T(8,128)(2,1)S(1)} %pad_maximum_fusion.2) | data formatting | bytes 8388608 | tf_op jit(solution)/shard_map/stack | solution.py:108
  82.5 99.9 %all_to_all.27 = bf16[2,256,4096]{1,0,2:T(2,128)(2,1)S(1)} all-to-all(bf16[2,256,4096]{1,0,2:T(2,128)(2,1)S(1)} %copy.105), channel_id=1, replica_groups=mesh['row'=2,'col'=8,'orient'=2] {'row','col'}, dimensions={2} | all-to-all | bytes 8388608 | tf_op jit(solution)/shard_map/all_to_all | solution.py:109
  216.7 6.8 fusion.34
  223.5 6.8 fusion.32
  230.3 7.2 %fusion.62 = bf16[256,128,32]{0,1,2:T(8,128)(2,1)S(1)} fusion(f32[256,32,128]{0,2,1:T(8,128)S(1)} %fusion.34, f32[256,32,128]{2,1,0:T(8,128)S(1)} %get-tuple-element.5), kind=kOutput, calls=%fused_computation.116 | convolution fusion | flops 1612939264 | bytes 10485760 | tf_op jit(solution)/shard_map/...kq,ql->...kl/dot_general | solution.py:89
  238.7 6.7 fusion.63
  247.0 27.2 %copy.116 = bf16[2,256,4096]{1,0,2:T(2,128)(2,1)} copy(bf16[2,256,4096]{1,2,0:T(8,128)(2,1)S(1)} %pad_maximum_fusion.3) | data formatting | bytes 8388608 | tf_op jit(solution)/shard_map/stack | solution.py:115
  298.7 74.4 %all-to-all-done.1 = bf16[2,256,4096]{1,0,2:T(2,128)(2,1)} async-done(((bf16[2,256,4096]{1,0,2:T(2,128)(2,1)}), bf16[2,256,4096]{1,0,2:T(2,128)(2,1)}, u32[]{:S(2)}, u32[]{:S(2)}) %all-to-all-start.1) | async-done | bytes 4194336 | tf_op jit(solution)/shard_map/all_to_all | solution.py:114
  412.2 12.7 %concatenate.10 = bf16[3,2064,512]{1,2,0:T(8,128)(2,1)} concatenate(bf16[3,8,512]{1,2,0:T(8,128)(2,1)} %copy-done.11, bf16[3,2048,512]{1,2,0:T(8,128)(2,1)} %copy-done.2, bf16[3,8,512]{1,2,0:T(8,128)(2,1)} %collective-permute-done.1), dimensions={1} | concatenate | bytes 12681216 | tf_op jit(solution)/shard_map/concatenate | solution.py:21
  444.1 6.7 fusion.18
  464.2 6.9 fusion.15
  471.1 6.7 fusion.14
  484.5 6.9 fusion.12
  498.1 6.7 fusion.10
  504.8 7.0 fusion.9
  511.9 6.7 fusion.8
  525.2 6.8 fusion.6
  532.1 6.7 fusion.5
  538.8 6.7 fusion.4
  552.2 51.8 %fusion = f32[4,128,2048,4,1,1]{2,1,5,4,3,0:T(8,128)} fusion(bf16[3,17,2048,4,144]{2,4,1,0,3:T(8,128)(2,1)} %fusion.3, bf16[2,4,17,144,128,1]{4,3,2,0,5,1:T(8,128)(2,1)} %maximum_bitcast_fusion.4), kind=kOutput, calls=%fused_computation.2 | convolution fusion | flops 41070624768 | bytes 102006784 | tf_op jit(solution)/shard_map/csxti,cfsio->fxto/dot_general | solution.py:163
  604.1 42.4 %fusion.2 = f32[128,2048,4]{1,0,2:T(8,128)} fusion(f32[4,128,2048,4,1,1]{2,1,5,4,3,0:T(8,128)} %fusion, bf16[3,17,2048,4,144]{2,4,1,0,3:T(8,128)(2,1)} %fusion.3, f32[4]{0:T(128)S(1)} %copy-done.16, f32[4]{0:T(128)S(1)} %copy-done.14, f32[4]{0:T(128)S(1)} %copy-done.20, f32[17,144,128]{2,1,0:T(8,128)S(1)} %copy-done.8, f32[4]{0:T(128)S(1)} %copy-done.22, ...), kind=kOutput, calls=%fused_computation.6 | convolution fusion | flops 20562706432 | bytes 62646420 | tf_op jit(solution)/shard_map/sxti,fsio->fxto/dot_general | solution.py:166
  656.6 45.4 %collective-permute-done.4 = f32[2048,256]{1,0:T(8,128)} collective-permute-done((f32[2048,256]{1,0:T(8,128)}, f32[2048,256]{1,0:T(8,128)}, u32[]{:S(2)}, u32[]{:S(2)}) %collective-permute-start.4) | collective-permute-done | bytes 2097184 | tf_op jit(solution)/shard_map/ppermute | solution.py:33
  (129 shorter events, 216.5 us)
Async XLA Ops:
  0.0 279.3 %copy-start = (f32[16,128,128]{2,1,0:T(8,128)S(1)}, f32[16,128,128]{2,1,0:T(8,128)}, u32[]{:S(2)}) copy-start(f32[16,128,128]{2,1,0:T(8,128)} %param.6) | copy-start | bytes 3145732
  274.2 98.9 %all-to-all-start.1 = ((bf16[2,256,4096]{1,0,2:T(2,128)(2,1)}), bf16[2,256,4096]{1,0,2:T(2,128)(2,1)}, u32[]{:S(2)}, u32[]{:S(2)}) async-start(bf16[2,256,4096]{1,0,2:T(2,128)(2,1)} %copy.116), calls=%async_computation.1 | async-start | bytes 8388608 | tf_op jit(solution)/shard_map/all_to_all | solution.py:114
  297.2 103.9 %copy-start.23 = (f32[17]{0:T(128)}, f32[17]{0:T(128)S(1)}, u32[]{:S(2)}) copy-start(f32[17]{0:T(128)S(1)} %add_convert_fusion.3) | copy-start | bytes 208
  297.3 103.8 %copy-start.9 = (pred[17,144,128]{2,1,0:T(8,128)(4,1)}, pred[17,144,128]{2,1,0:T(8,128)(4,1)S(1)}, u32[]{:S(2)}) copy-start(pred[17,144,128]{2,1,0:T(8,128)(4,1)S(1)} %fusion.76) | copy-start | bytes 940036
  298.6 102.5 %copy-start.13 = (f32[4]{0:T(128)}, f32[4]{0:T(128)S(1)}, u32[]{:S(2)}) copy-start(f32[4]{0:T(128)S(1)} %get-tuple-element.34) | copy-start | bytes 52
  298.6 102.5 %copy-start.15 = (f32[4]{0:T(128)}, f32[4]{0:T(128)S(1)}, u32[]{:S(2)}) copy-start(f32[4]{0:T(128)S(1)} %get-tuple-element.35) | copy-start | bytes 52
  298.6 102.5 %copy-start.17 = (f32[4]{0:T(128)}, f32[4]{0:T(128)S(1)}, u32[]{:S(2)}) copy-start(f32[4]{0:T(128)S(1)} %get-tuple-element.36) | copy-start | bytes 52
  298.6 102.5 %copy-start.19 = (f32[4]{0:T(128)}, f32[4]{0:T(128)S(1)}, u32[]{:S(2)}) copy-start(f32[4]{0:T(128)S(1)} %get-tuple-element.39) | copy-start | bytes 52
  298.6 102.5 %copy-start.21 = (f32[4]{0:T(128)}, f32[4]{0:T(128)S(1)}, u32[]{:S(2)}) copy-start(f32[4]{0:T(128)S(1)} %get-tuple-element.40) | copy-start | bytes 52
  389.7 11.5 %copy-start.7 = (f32[17,144,128]{2,1,0:T(8,128)S(1)}, f32[17,144,128]{2,1,0:T(8,128)}, u32[]{:S(2)}) copy-start(f32[17,144,128]{2,1,0:T(8,128)} %add_convert_fusion.2) | copy-start | bytes 3760132
  396.4 11.5 %collective-permute-start = (bf16[3,8,512]{1,2,0:T(8,128)(2,1)S(1)}, bf16[3,8,512]{1,2,0:T(8,128)(2,1)S(1)}, u32[]{:S(2)}, u32[]{:S(2)}) collective-permute-start(bf16[3,8,512]{1,2,0:T(8,128)(2,1)S(1)} %get-tuple-element.20), channel_id=1, source_target_pairs={{0,16},{1,17},{2,18},{3,19},{4,20},{5,21},{6,22},{7,23},{8,24},{9,... | collective-permute-start | bytes 73736 | tf_op jit(solution)/shard_map/ppermute | solution.py:23
  399.8 12.4 %collective-permute-start.1 = (bf16[3,8,512]{1,2,0:T(8,128)(2,1)S(1)}, bf16[3,8,512]{1,2,0:T(8,128)(2,1)}, u32[]{:S(2)}, u32[]{:S(2)}) collective-permute-start(bf16[3,8,512]{1,2,0:T(8,128)(2,1)S(1)} %get-tuple-element.19), channel_id=1, source_target_pairs={{16,0},{17,1},{18,2},{19,3},{20,4},{21,5},{22,6},{23,7},{24,8},{25... | collective-permute-start | bytes 73736 | tf_op jit(solution)/shard_map/ppermute | solution.py:25
  425.9 7.0 collective-permute-start.2
  427.2 5.7 collective-permute-start.3
  552.2 51.9 %copy-start.8 = (f32[17,144,128]{2,1,0:T(8,128)S(1)}, f32[17,144,128]{2,1,0:T(8,128)}, u32[]{:S(2)}) copy-start(f32[17,144,128]{2,1,0:T(8,128)} %add_convert_fusion.2) | copy-start | bytes 3760132
  552.2 51.9 %copy-start.10 = (pred[17,144,128]{2,1,0:T(8,128)(4,1)S(1)}, pred[17,144,128]{2,1,0:T(8,128)(4,1)}, u32[]{:S(2)}) copy-start(pred[17,144,128]{2,1,0:T(8,128)(4,1)} %copy-done.9) | copy-start | bytes 940036
  552.2 51.9 %copy-start.14 = (f32[4]{0:T(128)S(1)}, f32[4]{0:T(128)}, u32[]{:S(2)}) copy-start(f32[4]{0:T(128)} %copy-done.13) | copy-start | bytes 52
  552.2 51.9 %copy-start.16 = (f32[4]{0:T(128)S(1)}, f32[4]{0:T(128)}, u32[]{:S(2)}) copy-start(f32[4]{0:T(128)} %copy-done.15) | copy-start | bytes 52
  552.2 51.9 %copy-start.18 = (f32[4]{0:T(128)S(1)}, f32[4]{0:T(128)}, u32[]{:S(2)}) copy-start(f32[4]{0:T(128)} %copy-done.17) | copy-start | bytes 52
  552.2 51.9 %copy-start.20 = (f32[4]{0:T(128)S(1)}, f32[4]{0:T(128)}, u32[]{:S(2)}) copy-start(f32[4]{0:T(128)} %copy-done.19) | copy-start | bytes 52
  552.2 51.9 %copy-start.22 = (f32[4]{0:T(128)S(1)}, f32[4]{0:T(128)}, u32[]{:S(2)}) copy-start(f32[4]{0:T(128)} %copy-done.21) | copy-start | bytes 52
  552.2 51.9 %copy-start.24 = (f32[17]{0:T(128)S(1)}, f32[17]{0:T(128)}, u32[]{:S(2)}) copy-start(f32[17]{0:T(128)} %copy-done.23) | copy-start | bytes 208
  653.3 48.7 %collective-permute-start.4 = (f32[2048,256]{1,0:T(8,128)}, f32[2048,256]{1,0:T(8,128)}, u32[]{:S(2)}, u32[]{:S(2)}) collective-permute-start(f32[2048,256]{1,0:T(8,128)} %copy.147), channel_id=1, source_target_pairs={{0,1},{1,0},{2,3},{3,2},{4,5},{5,4},{6,7},{7,6},{8,9},{9,8},{10,11... | collective-permute-start | bytes 6291464 | tf_op jit(solution)/shard_map/ppermute | solution.py:33
  654.8 51.0 %copy-start.1 = (f32[16,128,128]{2,1,0:T(8,128)S(1)}, f32[16,128,128]{2,1,0:T(8,128)}, u32[]{:S(2)}) copy-start(f32[16,128,128]{2,1,0:T(8,128)} %param.6) | copy-start | bytes 3145732
  (9 other events, 32.9 us)
where the time goes:
time: 711 us; the launch traced here: 706 us
  local copies, waits for them, and re-layouts  243 us (34%)
  matrix products  178 us (25%)
  waiting for transfers between devices  125 us (18%)
  blocking collectives  99.9 us (14%)
  other arithmetic  45.5 us (6%)
  starting transfers between devices  13.6 us (2%)
    unnamed x75, local copies, waits for them, and re-layouts  122 us
    all_to_all x1, blocking collectives, body(): lax.all_to_all(spectrum.astype(jnp.bfloat16), ('row', 'col'), split_axis=...  99.9 us
    all_to_all x1, waiting for transfers between devices, body(): lax.all_to_all(jnp.stack([field_re, field_im]).astype(jnp.bfloat16), 'col...  74.4 us
    dot_general x1, matrix products, body(): jnp.einsum('csxti,cfsio->fxto', shifted[0:2], resist_kernel, preferred_el...  51.8 us
    ppermute x1, waiting for transfers between devices, partner(): lax.ppermute(x, axis, [(i, i ^ 1 << bit) for i in range(lax.axis_size(axi...  45.4 us
    dot_general x1, matrix products, body(): jnp.einsum('sxti,fsio->fxto', shifted[2], band_height, preferred_element_...  42.4 us
    another operation x1, local copies, waits for them, and re-layouts, body(): jnp.stack([field_re, field_im]).astype(jnp.bfloat16)  27.2 us
    another operation x1, local copies, waits for them, and re-layouts, body(): spectrum = jnp.stack([real_part, imag_part])  25.5 us
  transfers between devices with their start and end apart: 6, of which 4 were waited for; matrix products, arithmetic and copies ran while one was open for 4% of the time, Pallas kernels for 0%

commit v1 on v0

--- a/solution.py
+++ b/solution.py
@@ -10,6 +10,15 @@
 nugget_share = 0.3
 peak_share = 1024.0 / (2.0 * math.pi)
 cutoff_ratio = 32.0
+launch_the_slices = lambda state, dimension_no, dim_no: jnp.concatenate(
+    jax.lax.all_to_all(
+        jnp.stack(jnp.split(state, jax.lax.axis_size(("row", "col")), axis=dimension_no)),
+        ("row", "col"),
+        0,
+        0,
+    ),
+    axis=dim_no,
+)
 
 
 def extended(cells, sides, width):
@@ -106,9 +115,7 @@
     amplitudes = amplitude(u_index, v_index, side_cells)
     real_part, imag_part = transform_last(noise[0] * amplitudes, noise[1] * amplitudes)
     spectrum = jnp.stack([real_part, imag_part])
-    transposed = lax.all_to_all(
-        spectrum.astype(jnp.bfloat16), ("row", "col"), split_axis=2, concat_axis=1, tiled=True
-    ).astype(spectrum.dtype)
+    transposed = launch_the_slices(spectrum.astype(jnp.bfloat16), 2, 1).astype(spectrum.dtype)
     turned = jnp.swapaxes(transposed, 1, 2)
     field_re, field_im = transform_last(turned[0], turned[1])
     fields = lax.all_to_all(

time: 711 us -> 683 us (0.961)
  local copies, waits for them, and re-layouts: 243 us -> 215 us
    another operation x1 -> x0, local copies, waits for them, and re-layouts: 25.5 us -> none  [body(): spectrum = jnp.stack([real_part, imag_part])]
    all_to_all x2 -> x0, local copies, waits for them, and re-layouts: 8.77 us -> none  [body(): lax.all_to_all(spectrum.astype(jnp.bfloat16), ('row', 'col'), split_axis=...]
  transfers between devices with their start and end apart: 6 -> 6, of which waited for: 4 -> 4; matrix products, arithmetic and copies ran while one was open for 4% -> 5% of each run, Pallas kernels for 0% -> 0%
where the time goes in v1:
time: 683 us; the launch traced here: 678 us
  local copies, waits for them, and re-layouts  215 us (31%)
  matrix products  178 us (26%)
  waiting for transfers between devices  125 us (18%)
  blocking collectives  100 us (15%)
  other arithmetic  45.4 us (7%)
  starting transfers between devices  13.6 us (2%)
    unnamed x75, local copies, waits for them, and re-layouts  122 us
    all_to_all x1, blocking collectives, jax.lax.all_to_all(jnp.stack(jnp.split(state, jax.lax.axis_size(('row', '...  100 us
    all_to_all x1, waiting for transfers between devices, body(): lax.all_to_all(jnp.stack([field_re, field_im]).astype(jnp.bfloat16), 'col...  74.4 us
    dot_general x1, matrix products, body(): jnp.einsum('csxti,cfsio->fxto', shifted[0:2], resist_kernel, preferred_el...  51.8 us
    ppermute x1, waiting for transfers between devices, partner(): lax.ppermute(x, axis, [(i, i ^ 1 << bit) for i in range(lax.axis_size(axi...  45.4 us
    dot_general x1, matrix products, body(): jnp.einsum('sxti,fsio->fxto', shifted[2], band_height, preferred_element_...  42.4 us
    another operation x1, local copies, waits for them, and re-layouts, body(): jnp.stack([field_re, field_im]).astype(jnp.bfloat16)  27.2 us
    dot_general x2, matrix products, transform_last(): jnp.einsum('...kq,ql->...kl', imag_twist, inner_cos, precision=highest)  13.8 us
  transfers between devices with their start and end apart: 6, of which 4 were waited for; matrix products, arithmetic and copies ran while one was open for 5% of the time, Pallas kernels for 0%

profile of v1, /device:TPU:0, one launch (start us, length us, event | category | flops | bytes accessed | tf_op | source)
XLA Modules:
  0.0 678.2 jit_solution(12159289963111398564)
XLA Ops:
  33.8 7.0 %fusion.40 = f32[256,32,128]{0,2,1:T(8,128)S(1)} fusion(f32[256,32,128]{2,1,0:T(8,128)S(1)} %get-tuple-element.8), kind=kOutput, calls=%fused_computation.120 | convolution fusion | flops 1610842112 | bytes 8388608 | tf_op jit(solution)/shard_map/...kq,ql->...kl/dot_general | solution.py:101
  48.7 6.8 fusion.61
  57.1 100.0 %all_to_all.14 = bf16[16,2,256,256]{2,3,1,0:T(8,128)(2,1)} all-to-all(bf16[16,2,256,256]{2,3,1,0:T(8,128)(2,1)S(1)} %fusion.93), channel_id=1, replica_groups=mesh['row'=2,'col'=8,'orient'=2] {'row','col'}, dimensions={0} | all-to-all | bytes 8388608 | tf_op jit(solution)/shard_map/all_to_all | solution.py:14
  188.8 6.8 %fusion.34 = f32[256,32,128]{0,2,1:T(8,128)S(1)} fusion(f32[256,32,128]{2,1,0:T(8,128)S(1)} %get-tuple-element.6), kind=kOutput, calls=%fused_computation.114 | convolution fusion | flops 1610842112 | bytes 8388608 | tf_op jit(solution)/shard_map/...kq,ql->...kl/dot_general | solution.py:98
  195.6 6.8 fusion.32
  202.4 7.2 %fusion.62 = bf16[256,128,32]{0,1,2:T(8,128)(2,1)S(1)} fusion(f32[256,32,128]{0,2,1:T(8,128)S(1)} %fusion.34, f32[256,32,128]{2,1,0:T(8,128)S(1)} %get-tuple-element.5), kind=kOutput, calls=%fused_computation.145 | convolution fusion | flops 1612939264 | bytes 10485760 | tf_op jit(solution)/shard_map/...kq,ql->...kl/dot_general | solution.py:98
  210.8 6.7 fusion.63
  219.1 27.2 %copy.135 = bf16[2,256,4096]{1,0,2:T(2,128)(2,1)} copy(bf16[2,256,4096]{1,2,0:T(8,128)(2,1)S(1)} %pad_maximum_fusion.2) | data formatting | bytes 8388608 | tf_op jit(solution)/shard_map/stack | solution.py:122
  270.8 74.4 %all-to-all-done.1 = bf16[2,256,4096]{1,0,2:T(2,128)(2,1)} async-done(((bf16[2,256,4096]{1,0,2:T(2,128)(2,1)}), bf16[2,256,4096]{1,0,2:T(2,128)(2,1)}, u32[]{:S(2)}, u32[]{:S(2)}) %all-to-all-start.1) | async-done | bytes 4194336 | tf_op jit(solution)/shard_map/all_to_all | solution.py:121
  384.3 12.7 %concatenate.10 = bf16[3,2064,512]{1,2,0:T(8,128)(2,1)} concatenate(bf16[3,8,512]{1,2,0:T(8,128)(2,1)} %copy-done.11, bf16[3,2048,512]{1,2,0:T(8,128)(2,1)} %copy-done.2, bf16[3,8,512]{1,2,0:T(8,128)(2,1)} %collective-permute-done.1), dimensions={1} | concatenate | bytes 12681216 | tf_op jit(solution)/shard_map/concatenate | solution.py:30
  416.3 6.7 fusion.18
  423.0 6.7 fusion.17
  436.4 6.9 %fusion.15 = bf16[3,17,2048,4,144]{2,4,1,0,3:T(8,128)(2,1)} fusion(bf16[3,17,2048,4,144]{2,4,1,0,3:T(8,128)(2,1)} %fusion.16, bf16[3,2064,4,144]{1,3,0,2:T(8,128)(2,1)S(1)} %pad_maximum_fusion), kind=kLoop, calls=%fused_computation.64 | loop fusion | bytes 14155776
  443.2 6.7 fusion.14
  456.7 6.9 %fusion.12 = bf16[3,17,2048,4,144]{2,4,1,0,3:T(8,128)(2,1)} fusion(bf16[3,17,2048,4,144]{2,4,1,0,3:T(8,128)(2,1)} %fusion.13, bf16[3,2064,4,144]{1,3,0,2:T(8,128)(2,1)S(1)} %pad_maximum_fusion), kind=kLoop, calls=%fused_computation.58 | loop fusion | bytes 14155776
  470.2 6.7 fusion.10
  477.0 7.0 %fusion.9 = bf16[3,17,2048,4,144]{2,4,1,0,3:T(8,128)(2,1)} fusion(bf16[3,17,2048,4,144]{2,4,1,0,3:T(8,128)(2,1)} %fusion.10, bf16[3,2064,4,144]{1,3,0,2:T(8,128)(2,1)S(1)} %pad_maximum_fusion), kind=kLoop, calls=%fused_computation.52 | loop fusion | bytes 14155776
  484.0 6.7 fusion.8
  497.4 6.8 %fusion.6 = bf16[3,17,2048,4,144]{2,4,1,0,3:T(8,128)(2,1)} fusion(bf16[3,17,2048,4,144]{2,4,1,0,3:T(8,128)(2,1)} %fusion.7, bf16[3,2064,4,144]{1,3,0,2:T(8,128)(2,1)S(1)} %pad_maximum_fusion), kind=kLoop, calls=%fused_computation.46 | loop fusion | bytes 14155776
  504.2 6.7 fusion.5
  510.9 6.7 fusion.4
  524.4 51.8 %fusion = f32[4,128,2048,4,1,1]{2,1,5,4,3,0:T(8,128)} fusion(bf16[3,17,2048,4,144]{2,4,1,0,3:T(8,128)(2,1)} %fusion.3, bf16[2,4,17,144,128,1]{4,3,2,0,5,1:T(8,128)(2,1)} %maximum_bitcast_fusion.4), kind=kOutput, calls=%fused_computation.2 | convolution fusion | flops 41070624768 | bytes 102006784 | tf_op jit(solution)/shard_map/csxti,cfsio->fxto/dot_general | solution.py:170
  576.2 42.4 %fusion.2 = f32[128,2048,4]{1,0,2:T(8,128)} fusion(f32[4,128,2048,4,1,1]{2,1,5,4,3,0:T(8,128)} %fusion, bf16[3,17,2048,4,144]{2,4,1,0,3:T(8,128)(2,1)} %fusion.3, f32[4]{0:T(128)S(1)} %copy-done.16, f32[4]{0:T(128)S(1)} %copy-done.14, f32[4]{0:T(128)S(1)} %copy-done.20, f32[17,144,128]{2,1,0:T(8,128)S(1)} %copy-done.8, f32[4]{0:T(128)S(1)} %copy-done.22, ...), kind=kOutput, calls=%fused_computation.6 | convolution fusion | flops 20562706432 | bytes 62646420 | tf_op jit(solution)/shard_map/sxti,fsio->fxto/dot_general | solution.py:173
  628.8 45.4 %collective-permute-done.4 = f32[2048,256]{1,0:T(8,128)} collective-permute-done((f32[2048,256]{1,0:T(8,128)}, f32[2048,256]{1,0:T(8,128)}, u32[]{:S(2)}, u32[]{:S(2)}) %collective-permute-start.4) | collective-permute-done | bytes 2097184 | tf_op jit(solution)/shard_map/ppermute | solution.py:42
  (142 shorter events, 207.2 us)
Async XLA Ops:
  0.0 251.4 %copy-start = (f32[16,128,128]{2,1,0:T(8,128)S(1)}, f32[16,128,128]{2,1,0:T(8,128)}, u32[]{:S(2)}) copy-start(f32[16,128,128]{2,1,0:T(8,128)} %param.6) | copy-start | bytes 3145732
  246.4 98.9 %all-to-all-start.1 = ((bf16[2,256,4096]{1,0,2:T(2,128)(2,1)}), bf16[2,256,4096]{1,0,2:T(2,128)(2,1)}, u32[]{:S(2)}, u32[]{:S(2)}) async-start(bf16[2,256,4096]{1,0,2:T(2,128)(2,1)} %copy.135), calls=%async_computation.1 | async-start | bytes 8388608 | tf_op jit(solution)/shard_map/all_to_all | solution.py:121
  269.3 103.9 %copy-start.23 = (f32[17]{0:T(128)}, f32[17]{0:T(128)S(1)}, u32[]{:S(2)}) copy-start(f32[17]{0:T(128)S(1)} %add_convert_fusion.3) | copy-start | bytes 208
  269.4 103.8 %copy-start.9 = (pred[17,144,128]{2,1,0:T(8,128)(4,1)}, pred[17,144,128]{2,1,0:T(8,128)(4,1)S(1)}, u32[]{:S(2)}) copy-start(pred[17,144,128]{2,1,0:T(8,128)(4,1)S(1)} %fusion.76) | copy-start | bytes 940036
  270.7 102.6 %copy-start.13 = (f32[4]{0:T(128)}, f32[4]{0:T(128)S(1)}, u32[]{:S(2)}) copy-start(f32[4]{0:T(128)S(1)} %get-tuple-element.34) | copy-start | bytes 52
  270.7 102.6 %copy-start.15 = (f32[4]{0:T(128)}, f32[4]{0:T(128)S(1)}, u32[]{:S(2)}) copy-start(f32[4]{0:T(128)S(1)} %get-tuple-element.35) | copy-start | bytes 52
  270.7 102.6 %copy-start.17 = (f32[4]{0:T(128)}, f32[4]{0:T(128)S(1)}, u32[]{:S(2)}) copy-start(f32[4]{0:T(128)S(1)} %get-tuple-element.36) | copy-start | bytes 52
  270.7 102.6 %copy-start.19 = (f32[4]{0:T(128)}, f32[4]{0:T(128)S(1)}, u32[]{:S(2)}) copy-start(f32[4]{0:T(128)S(1)} %get-tuple-element.39) | copy-start | bytes 52
  270.8 102.6 %copy-start.21 = (f32[4]{0:T(128)}, f32[4]{0:T(128)S(1)}, u32[]{:S(2)}) copy-start(f32[4]{0:T(128)S(1)} %get-tuple-element.40) | copy-start | bytes 52
  361.8 11.5 %copy-start.7 = (f32[17,144,128]{2,1,0:T(8,128)S(1)}, f32[17,144,128]{2,1,0:T(8,128)}, u32[]{:S(2)}) copy-start(f32[17,144,128]{2,1,0:T(8,128)} %add_convert_fusion.2) | copy-start | bytes 3760132
  368.5 11.6 %collective-permute-start = (bf16[3,8,512]{1,2,0:T(8,128)(2,1)S(1)}, bf16[3,8,512]{1,2,0:T(8,128)(2,1)S(1)}, u32[]{:S(2)}, u32[]{:S(2)}) collective-permute-start(bf16[3,8,512]{1,2,0:T(8,128)(2,1)S(1)} %get-tuple-element.20), channel_id=1, source_target_pairs={{0,16},{1,17},{2,18},{3,19},{4,20},{5,21},{6,22},{7,23},{8,24},{9,... | collective-permute-start | bytes 73736 | tf_op jit(solution)/shard_map/ppermute | solution.py:32
  371.9 12.4 %collective-permute-start.1 = (bf16[3,8,512]{1,2,0:T(8,128)(2,1)S(1)}, bf16[3,8,512]{1,2,0:T(8,128)(2,1)}, u32[]{:S(2)}, u32[]{:S(2)}) collective-permute-start(bf16[3,8,512]{1,2,0:T(8,128)(2,1)S(1)} %get-tuple-element.19), channel_id=1, source_target_pairs={{16,0},{17,1},{18,2},{19,3},{20,4},{21,5},{22,6},{23,7},{24,8},{25... | collective-permute-start | bytes 73736 | tf_op jit(solution)/shard_map/ppermute | solution.py:34
  398.0 7.0 %collective-permute-start.2 = (bf16[3,2064,8]{1,2,0:T(8,128)(2,1)S(1)}, bf16[3,2064,8]{1,2,0:T(8,128)(2,1)S(1)}, u32[]{:S(2)}, u32[]{:S(2)}) collective-permute-start(bf16[3,2064,8]{1,2,0:T(8,128)(2,1)S(1)} %get-tuple-element.17), channel_id=1, source_target_pairs={{0,2},{2,4},{4,6},{6,8},{8,10},{10,12},{12,14},{1,3},{3,5},{5,7},{... | collective-permute-start | bytes 297224 | tf_op jit(solution)/shard_map/ppermute | solution.py:32
  399.3 5.7 collective-permute-start.3
  524.3 51.9 %copy-start.8 = (f32[17,144,128]{2,1,0:T(8,128)S(1)}, f32[17,144,128]{2,1,0:T(8,128)}, u32[]{:S(2)}) copy-start(f32[17,144,128]{2,1,0:T(8,128)} %add_convert_fusion.2) | copy-start | bytes 3760132
  524.3 51.9 %copy-start.10 = (pred[17,144,128]{2,1,0:T(8,128)(4,1)S(1)}, pred[17,144,128]{2,1,0:T(8,128)(4,1)}, u32[]{:S(2)}) copy-start(pred[17,144,128]{2,1,0:T(8,128)(4,1)} %copy-done.9) | copy-start | bytes 940036
  524.3 51.9 %copy-start.14 = (f32[4]{0:T(128)S(1)}, f32[4]{0:T(128)}, u32[]{:S(2)}) copy-start(f32[4]{0:T(128)} %copy-done.13) | copy-start | bytes 52
  524.3 51.9 %copy-start.16 = (f32[4]{0:T(128)S(1)}, f32[4]{0:T(128)}, u32[]{:S(2)}) copy-start(f32[4]{0:T(128)} %copy-done.15) | copy-start | bytes 52
  524.3 51.9 %copy-start.18 = (f32[4]{0:T(128)S(1)}, f32[4]{0:T(128)}, u32[]{:S(2)}) copy-start(f32[4]{0:T(128)} %copy-done.17) | copy-start | bytes 52
  524.3 51.9 %copy-start.20 = (f32[4]{0:T(128)S(1)}, f32[4]{0:T(128)}, u32[]{:S(2)}) copy-start(f32[4]{0:T(128)} %copy-done.19) | copy-start | bytes 52
  524.3 51.9 %copy-start.22 = (f32[4]{0:T(128)S(1)}, f32[4]{0:T(128)}, u32[]{:S(2)}) copy-start(f32[4]{0:T(128)} %copy-done.21) | copy-start | bytes 52
  524.3 51.9 %copy-start.24 = (f32[17]{0:T(128)S(1)}, f32[17]{0:T(128)}, u32[]{:S(2)}) copy-start(f32[17]{0:T(128)} %copy-done.23) | copy-start | bytes 208
  625.5 48.7 %collective-permute-start.4 = (f32[2048,256]{1,0:T(8,128)}, f32[2048,256]{1,0:T(8,128)}, u32[]{:S(2)}, u32[]{:S(2)}) collective-permute-start(f32[2048,256]{1,0:T(8,128)} %copy.167), channel_id=1, source_target_pairs={{0,1},{1,0},{2,3},{3,2},{4,5},{5,4},{6,7},{7,6},{8,9},{9,8},{10,11... | collective-permute-start | bytes 6291464 | tf_op jit(solution)/shard_map/ppermute | solution.py:42
  627.0 51.0 %copy-start.1 = (f32[16,128,128]{2,1,0:T(8,128)S(1)}, f32[16,128,128]{2,1,0:T(8,128)}, u32[]{:S(2)}) copy-start(f32[16,128,128]{2,1,0:T(8,128)} %param.6) | copy-start | bytes 3145732
  (9 other events, 32.8 us)
